TPU v7x, 32 devices: a whole 2x2x4 slice. The times are simulated.
32 devices in a mesh: dp: 8 (over y, x, core), tensor: 4 (over z).
Axes of the slice: x: 2, y: 2, z: 4, core: 2. Of those that a mesh axis runs over, the one named last changes fastest.
Arguments:
- tokens: bfloat16 [32, 1024, 512], P(('dp', 'tensor')), may hold values from -6 to 6
- timestep: int32 [32], P(('dp', 'tensor')), may hold values from 0 to 999
- segment_ids: int32 [32, 1024], P('dp'), may hold values from 0 to 7, never falling along the last dimension, each value on 1 to 512 neighbouring positions
- span_lengths: int32 [32], P('dp'), may hold values from 512 to 1024
- w_qkv: float32 [3, 512, 512], P(None, 'dp', 'tensor'), may hold values from -0.25 to 0.25
- w_out_t: float32 [512, 512], P('dp', 'tensor'), may hold values from -1.5 to 1.5
- w_up: float32 [512, 2048], P('dp', 'tensor'), may hold values from -0.25 to 0.25
- w_down_t: float32 [512, 2048], P('dp', 'tensor'), may hold values from -0.125 to 0.125
- w_time: float32 [512, 512], replicated, may hold values from -0.25 to 0.25
- b_time: float32 [512], replicated, may hold values from -3 to 3
- ln1_gain: float32 [512], replicated, may hold values from 0.1 to 1.9
- ln1_bias: float32 [512], replicated, may hold values from -3 to 3
- ln2_gain: float32 [512], replicated, may hold values from 0.1 to 1.9
- ln2_bias: float32 [512], replicated, may hold values from -3 to 3
- b_up: float32 [2048], replicated, may hold values from -3 to 3
- b_down: float32 [512], replicated, may hold values from -3 to 3
- cotangent: bfloat16 [32, 1024, 512], P(('dp', 'tensor')), may hold values from -6 to 6
Outputs:
- layer_out: bfloat16 [32, 1024, 512], P(('dp', 'tensor'))
- grad_tokens: float32 [32, 1024, 512], P(('dp', 'tensor'))
- grad_w_qkv: float32 [3, 512, 512], P(None, 'dp', 'tensor')
- grad_w_out_t: float32 [512, 512], P('dp', 'tensor')
- grad_w_up: float32 [512, 2048], P('dp', 'tensor')
- grad_w_down_t: float32 [512, 2048], P('dp', 'tensor')
- grad_w_time: float32 [512, 512], replicated
- grad_b_time: float32 [512], replicated
- grad_ln1_gain: float32 [512], replicated
- grad_ln1_bias: float32 [512], replicated
- grad_ln2_gain: float32 [512], replicated
- grad_ln2_bias: float32 [512], replicated
- grad_b_up: float32 [2048], replicated
- grad_b_down: float32 [512], replicated
Inputs may be any that keep to these rules, and one draw needn't show every extreme that they name: `segment_ids`: never falls along a row; each document has 1 to 512 positions and one has exactly that many.
All inputs are finite; a program needn't handle non-finite values.
Results may differ from a plain program's by a relative error of at most 0.013.
Values may be sent and summed in bfloat16 or wider, within the bound.
A program may use at most 192 MiB of HBM per device.

v0:
```python
import math
import jax
import jax.numpy as jnp
from jax import lax
from jax.sharding import PartitionSpec as P

HS = 64
FF = 2048
highest = lax.Precision.HIGHEST
epsilon = 1e-05
masked_score = -1e30


def split_up(value, dim, count):
    before, after = (value.shape[:dim], value.shape[dim + 1 :])
    return jnp.moveaxis(value.reshape(*before, count, -1, *after), dim, 0)


def sent_and_summed(value, axis, dim):
    count = lax.axis_size(axis)
    parts = lax.all_to_all(split_up(value, dim, count), axis, 0, 0, tiled=True)
    return jnp.sum(parts.astype(jnp.float32), axis=0)


def side_by_side(arrays, axis, dim, along):
    ends, at = ([], 0)
    for a in arrays[:-1]:
        at += a.shape[along]
        ends.append(at)
    both = jnp.concatenate(arrays, axis=along)
    return tuple(jnp.split(sent_and_summed(both, axis, dim), ends, axis=along))


def norm_layer(values, gain_vec, shift_vec):
    row_mean = jnp.mean(values, axis=-1, keepdims=True)
    centred = values - row_mean
    variance = jnp.mean(centred * centred, axis=-1, keepdims=True)
    return centred * lax.rsqrt(variance + epsilon) * gain_vec + shift_vec


def time_features(timestep, features):
    half_width = features // 2
    frequency = jnp.exp(-math.log(10000.0) * jnp.arange(half_width, dtype=jnp.float32) / half_width)
    angles = timestep.astype(jnp.float32)[:, None] * frequency[None, :]
    return jnp.concatenate([jnp.sin(angles), jnp.cos(angles)], axis=1)


def allowed_keys(segment, length):
    places = jnp.arange(segment.shape[0], dtype=jnp.int32)
    same_doc = segment[:, None] == segment[None, :]
    is_valid = (places < length)[None, :] | (places[:, None] == places[None, :])
    return same_doc & is_valid


def gelu_tanh(values):
    return jax.nn.gelu(values, approximate=True)


def split_heads(values):
    return values.reshape(values.shape[0], values.shape[1] // HS, HS)


def head_scores(query_heads, key_heads, allowed):
    scores = jnp.einsum(
        "qhe,khe->hqk", query_heads, key_heads, preferred_element_type=jnp.float32
    ) * (1.0 / math.sqrt(HS))
    return jnp.where(allowed[None], scores, masked_score)


def attend_forward(packed):
    query_heads = split_heads(packed[0])
    key_heads = split_heads(packed[1])
    value_heads = split_heads(packed[2])
    scores = head_scores(query_heads, key_heads, allowed_keys(packed[3], packed[4]))
    row_max = jnp.max(scores, axis=-1, keepdims=True)
    raised = jnp.exp(scores - row_max)
    row_total = jnp.sum(raised, axis=-1, keepdims=True)
    probs_low = (raised / row_total).astype(jnp.bfloat16)
    mixed = jnp.einsum("hqk,khe->qhe", probs_low, value_heads, preferred_element_type=jnp.float32)
    return (mixed.reshape(packed[0].shape).astype(jnp.bfloat16), row_max + jnp.log(row_total))


def attend_backward(packed):
    query_heads = split_heads(packed[0])
    key_heads = split_heads(packed[1])
    value_heads = split_heads(packed[2])
    grad_heads = split_heads(packed[3])
    scores = head_scores(query_heads, key_heads, allowed_keys(packed[5], packed[6]))
    attn_probs = jnp.exp(scores - packed[4])
    probs_low = attn_probs.astype(jnp.bfloat16)
    grad_values = jnp.einsum(
        "hqk,qhe->khe", probs_low, grad_heads, preferred_element_type=jnp.float32
    )
    grad_probs = jnp.einsum(
        "qhe,khe->hqk", grad_heads, value_heads, preferred_element_type=jnp.float32
    )
    row_delta = jnp.sum(attn_probs * grad_probs, axis=-1, keepdims=True)
    grad_scores = (attn_probs * (grad_probs - row_delta)).astype(jnp.bfloat16)
    score_scale = 1.0 / math.sqrt(HS)
    grad_queries = (
        jnp.einsum("hqk,khe->qhe", grad_scores, key_heads, preferred_element_type=jnp.float32)
        * score_scale
    )
    grad_keys = (
        jnp.einsum("hqk,qhe->khe", grad_scores, query_heads, preferred_element_type=jnp.float32)
        * score_scale
    )
    shape_rows = packed[0].shape
    return jnp.stack(
        [
            grad_queries.reshape(shape_rows),
            grad_keys.reshape(shape_rows),
            grad_values.reshape(shape_rows),
        ]
    ).astype(jnp.bfloat16)


def shards(
    tokens,
    timestep,
    segment_ids,
    span_lengths,
    w_qkv,
    w_out_t,
    w_up,
    w_down_t,
    w_time,
    b_time,
    ln1_gain,
    ln1_bias,
    ln2_gain,
    ln2_bias,
    b_up,
    b_down,
    cotangent,
):
    tensor_place = lax.axis_index("tensor")
    qkv_copy, out_copy, up_copy, down_copy = (
        lax.all_gather(w_qkv.astype(jnp.bfloat16), "dp", axis=1, tiled=True),
        lax.all_gather(w_out_t.astype(jnp.bfloat16), "dp", axis=0, tiled=True),
        lax.all_gather(w_up.astype(jnp.bfloat16), "dp", axis=0, tiled=True),
        lax.all_gather(w_down_t.astype(jnp.bfloat16), "dp", axis=0, tiled=True),
    )
    bias_up_cols = lax.dynamic_slice_in_dim(
        b_up, tensor_place * up_copy.shape[1], up_copy.shape[1], 0
    )
    ff_cols = up_copy.shape[1]
    time_emb = time_features(timestep, tokens.shape[2])
    time_proj = jnp.dot(time_emb, w_time, precision=highest) + b_time
    start = tokens.astype(jnp.float32) + time_proj[:, None, :]
    normed_one = norm_layer(start, ln1_gain, ln1_bias).astype(jnp.bfloat16)
    normed_all = lax.all_gather(normed_one, "tensor", axis=0, tiled=True)
    qkv_act = jnp.einsum(
        "nsd,cde->cnse", normed_all, qkv_copy, preferred_element_type=jnp.float32
    ).astype(jnp.bfloat16)
    mixed, log_total = lax.map(
        attend_forward, (qkv_act[0], qkv_act[1], qkv_act[2], segment_ids, span_lengths)
    )
    part_rows = mixed
    attn_out = lax.psum_scatter(
        jnp.einsum("nse,de->nsd", part_rows, out_copy, preferred_element_type=jnp.float32),
        "tensor",
        scatter_dimension=0,
        tiled=True,
    )
    middle = start + attn_out
    normed_two = norm_layer(middle, ln2_gain, ln2_bias).astype(jnp.bfloat16)
    second_all = lax.all_gather(normed_two, "tensor", axis=0, tiled=True)
    upper = (
        jnp.einsum("nsd,df->nsf", second_all, up_copy, preferred_element_type=jnp.float32)
        + bias_up_cols
    )
    activated = gelu_tanh(upper).astype(jnp.bfloat16)
    part_rows = activated
    ffn_out = lax.psum_scatter(
        jnp.einsum("nsf,df->nsd", part_rows, down_copy, preferred_element_type=jnp.float32).astype(
            jnp.bfloat16
        ),
        "tensor",
        scatter_dimension=0,
        tiled=True,
    ).astype(jnp.float32)
    layer_out = (middle + ffn_out + b_down).astype(jnp.bfloat16)
    grad_b_down = jnp.sum(cotangent.astype(jnp.float32), axis=(0, 1))
    grad_out_all = lax.all_gather(cotangent, "tensor", axis=0, tiled=True)
    grad_down = jnp.einsum(
        "nsd,nsf->df", grad_out_all, activated, preferred_element_type=jnp.float32
    )
    grad_act = jnp.einsum(
        "nsd,df->nsf", grad_out_all, down_copy, preferred_element_type=jnp.float32
    )
    gelu_value, gelu_pull = jax.vjp(gelu_tanh, upper)
    grad_upper = gelu_pull(grad_act)[0].astype(jnp.bfloat16)
    grad_bias_cols = jnp.sum(grad_upper.astype(jnp.float32), axis=(0, 1))
    grad_up = jnp.einsum("nsd,nsf->df", second_all, grad_upper, preferred_element_type=jnp.float32)
    part_rows = grad_upper
    grad_normed_two = lax.psum_scatter(
        jnp.einsum("nsf,df->nsd", part_rows, up_copy, preferred_element_type=jnp.float32).astype(
            jnp.bfloat16
        ),
        "tensor",
        scatter_dimension=0,
        tiled=True,
    ).astype(jnp.float32)
    norm_two_value, norm_two_pull = jax.vjp(norm_layer, middle, ln2_gain, ln2_bias)
    grad_middle_norm, grad_gain_two, grad_bias_two = norm_two_pull(grad_normed_two)
    grad_middle = cotangent.astype(jnp.float32) + grad_middle_norm
    grad_attn = grad_middle.astype(jnp.bfloat16)
    grad_attn_all = lax.all_gather(grad_attn, "tensor", axis=0, tiled=True)
    grad_out_w = jnp.einsum("nsd,nse->de", grad_attn_all, mixed, preferred_element_type=jnp.float32)
    grad_mixed = jnp.einsum(
        "nsd,de->nse", grad_attn_all, out_copy, preferred_element_type=jnp.float32
    ).astype(jnp.bfloat16)
    grad_qkv_act = lax.map(
        attend_backward,
        (qkv_act[0], qkv_act[1], qkv_act[2], grad_mixed, log_total, segment_ids, span_lengths),
    )
    grad_qkv_w = jnp.einsum(
        "nsd,ncse->cde", normed_all, grad_qkv_act, preferred_element_type=jnp.float32
    )
    part_rows = grad_qkv_act
    grad_normed_one = lax.psum_scatter(
        jnp.einsum("ncse,cde->nsd", part_rows, qkv_copy, preferred_element_type=jnp.float32).astype(
            jnp.bfloat16
        ),
        "tensor",
        scatter_dimension=0,
        tiled=True,
    ).astype(jnp.float32)
    norm_one_value, norm_one_pull = jax.vjp(norm_layer, start, ln1_gain, ln1_bias)
    grad_start_norm, grad_gain_one, grad_bias_one = norm_one_pull(grad_normed_one)
    grad_tokens = grad_middle + grad_start_norm
    grad_time_rows = jnp.sum(grad_tokens, axis=1)
    grad_time_w = jnp.dot(time_emb.T, grad_time_rows, precision=highest)
    grad_time_bias = jnp.sum(grad_time_rows, axis=0)
    grad_bias_up = lax.dynamic_update_slice_in_dim(
        jnp.zeros((FF,), jnp.float32), grad_bias_cols, tensor_place * ff_cols, 0
    )
    shard_qkv, shard_out, shard_up, shard_down = (
        sent_and_summed(grad_qkv_w.astype(jnp.bfloat16), "dp", 1),
        *side_by_side(
            (
                grad_out_w.astype(jnp.bfloat16),
                grad_up.astype(jnp.bfloat16),
                grad_down.astype(jnp.bfloat16),
            ),
            "dp",
            0,
            1,
        ),
    )
    summed = lax.psum(
        (
            grad_time_w,
            grad_time_bias,
            grad_gain_one,
            grad_bias_one,
            grad_gain_two,
            grad_bias_two,
            grad_bias_up,
            grad_b_down,
        ),
        ("dp", "tensor"),
    )
    return (
        layer_out,
        grad_tokens,
        shard_qkv,
        shard_out,
        shard_up,
        shard_down,
        summed[0],
        summed[1],
        summed[2],
        summed[3],
        summed[4],
        summed[5],
        summed[6],
        summed[7],
    )


def solution(mesh):
    return jax.shard_map(
        shards,
        mesh=mesh,
        in_specs=(
            P(("dp", "tensor"), None, None),
            P(("dp", "tensor")),
            P("dp", None),
            P("dp"),
            P(None, "dp", "tensor"),
            P("dp", "tensor"),
            P("dp", "tensor"),
            P("dp", "tensor"),
            P(),
            P(),
            P(),
            P(),
            P(),
            P(),
            P(),
            P(),
            P(("dp", "tensor"), None, None),
        ),
        out_specs=(
            P(("dp", "tensor"), None, None),
            P(("dp", "tensor"), None, None),
            P(None, "dp", "tensor"),
            P("dp", "tensor"),
            P("dp", "tensor"),
            P("dp", "tensor"),
            P(),
            P(),
            P(),
            P(),
            P(),
            P(),
            P(),
            P(),
        ),
        check_vma=False,
    )
```

profile of v0, /device:TPU:0, one launch (start us, length us, event | category | flops | bytes accessed | tf_op | source)
XLA Modules:
  0.0 1040.7 jit_solution(14734776910179383602)
XLA Ops:
  11.3 1.7 multiply_reduce_fusion.2
  13.0 2.7 add_convert_fusion.2
  15.9 10.7 %all_gather.26 = bf16[512,128]{1,0:T(8,128)(2,1)S(1)} all-gather(bf16[64,128]{1,0:T(8,128)(2,1)S(1)} %convert_element_type.133), channel_id=1, replica_groups=mesh['dp'=8,'tensor'=4] {'dp'}, dimensions={0}, use_global_device_ids=true | all-gather | bytes 147456 | tf_op jit(solution)/shard_map/all_gather | solution.py:140
  26.6 9.7 all_gather.25
  36.3 63.1 %all-gather.5.cloned.1.call-done = bf16[4,1024,512]{2,1,0:T(8,128)(2,1)} async-done(((bf16[1,1024,512]{2,1,0:T(8,128)(2,1)}), bf16[4,1024,512]{2,1,0:T(8,128)(2,1)}) %all-gather.5.cloned.1.call-update) | async-done | bytes 4194320 | tf_op jit(solution)/shard_map/all_gather | solution.py:152
  99.4 4.5 convert_bitcast_fusion
  109.8 42.4 %while.22 = (s32[]{:T(128)}, bf16[4,1024,128]{1,2,0:T(8,128)(2,1)S(1)}, f32[4,2,1024,1]{2,1,3,0:T(2,128)S(1)}, bf16[4,1024,128]{1,2,0:T(8,128)(2,1)S(1)}, s32[4,...) while((s32[]{:T(128)}, ...), condition=%wide.region_5.6_spmd, body=%wide.region_2.5_spmd.sunk | while | flops 566361088 | bytes 32585864 | solution.py:156
  113.6 1.9 fusion.134
  115.5 2.0 fusion.135
  117.5 2.8 fusion.136
  124.2 1.9 fusion.134
  126.1 2.0 fusion.135
  128.1 2.8 fusion.136
  134.8 1.9 fusion.134
  136.7 2.0 fusion.135
  138.7 2.8 fusion.136
  145.4 1.9 fusion.134
  147.3 2.0 fusion.135
  149.3 2.8 fusion.136
  152.2 4.5 fusion.69
  156.9 143.1 %reduce-scatter.5.cloned.1.call-done = f32[1,1024,512]{2,1,0:T(8,128)} async-done(((f32[4,1024,512]{2,1,0:T(8,128)}), f32[1,1024,512]{2,1,0:T(8,128)}) %reduce-scatter.5.cloned.1.call-update) | async-done | bytes 2097168 | tf_op jit(solution)/shard_map/reduce_scatter | solution.py:160
  299.9 1.9 fusion.79
  305.2 10.2 all_gather.29
  315.4 9.8 all_gather.28
  325.2 60.2 %all-gather.7.cloned.1.call-done = bf16[4,1024,512]{2,1,0:T(8,128)(2,1)} async-done(((bf16[1,1024,512]{2,1,0:T(8,128)(2,1)}), bf16[4,1024,512]{2,1,0:T(8,128)(2,1)}) %all-gather.7.cloned.1.call-update) | async-done | bytes 4194320 | tf_op jit(solution)/shard_map/all_gather | solution.py:168
  385.5 8.0 fusion.64
  393.4 72.8 %all-gather.9.cloned.1.call-done = bf16[4,1024,512]{2,1,0:T(8,128)(2,1)} async-done(((bf16[1,1024,512]{2,1,0:T(8,128)(2,1)}), bf16[4,1024,512]{2,1,0:T(8,128)(2,1)}) %all-gather.9.cloned.1.call-update) | async-done | bytes 4194320 | tf_op jit(solution)/shard_map/all_gather | solution.py:185
  466.2 10.3 convert_reduce_fusion
  476.5 2.0 copy-done.47
  478.5 4.5 convolution_convert_fusion
  483.1 8.8 convolution_convert_fusion.1
  491.9 66.5 %reduce-scatter.9.cloned.1.call-done = bf16[1,1024,512]{2,1,0:T(8,128)(2,1)} async-done(((bf16[4,1024,512]{2,1,0:T(8,128)(2,1)}), bf16[1,1024,512]{2,1,0:T(8,128)(2,1)}) %reduce-scatter.9.cloned.1.call-update) | async-done | bytes 1048592 | tf_op jit(solution)/shard_map/reduce_scatter | solution.py:197
  558.5 2.7 fusion.40
  561.2 76.8 %reduce-scatter.7.cloned.1.call-done = bf16[1,1024,512]{2,1,0:T(8,128)(2,1)} async-done(((bf16[4,1024,512]{2,1,0:T(8,128)(2,1)}), bf16[1,1024,512]{2,1,0:T(8,128)(2,1)}) %reduce-scatter.7.cloned.1.call-update) | async-done | bytes 1048592 | tf_op jit(solution)/shard_map/reduce_scatter | solution.py:175
  638.0 3.2 fusion.78
  644.2 81.2 %all-gather.11.cloned.1.call-done = bf16[4,1024,512]{2,1,0:T(8,128)(2,1)} async-done(((bf16[1,1024,512]{2,1,0:T(8,128)(2,1)}), bf16[4,1024,512]{2,1,0:T(8,128)(2,1)}) %all-gather.11.cloned.1.call-update) | async-done | bytes 4194320 | tf_op jit(solution)/shard_map/all_gather | solution.py:209
  725.3 3.4 convolution_convert_fusion.2
  728.8 72.6 %while.23 = (s32[]{:T(128)}, bf16[4,3,1024,128]{2,3,1,0:T(8,128)(2,1)}, bf16[4,1024,128]{1,2,0:T(8,128)(2,1)}, s32[4,1024]{1,0:T(4,128)S(1)}, s32[4]{0:T(128)S(1...) while((s32[]{:T(128)}, ...), condition=%wide.region_15.16_spmd, body=%wide.region_13.15_spmd.sunk | while | flops 1380842496 | bytes 73996440 | solution.py:214
  735.1 2.5 fusion.149
  737.6 3.4 multiply_reduce_fusion.4
  741.1 2.7 multiply_convert_fusion.5
  753.3 2.5 fusion.149
  755.8 3.4 multiply_reduce_fusion.4
  759.2 2.7 multiply_convert_fusion.5
  771.4 2.5 fusion.149
  773.9 3.4 multiply_reduce_fusion.4
  777.4 2.7 multiply_convert_fusion.5
  789.6 2.5 fusion.149
  792.1 3.4 multiply_reduce_fusion.4
  795.5 2.7 multiply_convert_fusion.5
  801.4 6.3 bitcast_convert_fusion
  809.3 6.5 fusion.47
  815.9 7.1 fusion.55
  825.3 5.1 fusion.57
  831.4 3.8 all-to-all-start
  835.2 47.9 %reduce-scatter.11.cloned.1.call-done = bf16[1,1024,512]{2,1,0:T(8,128)(2,1)} async-done(((bf16[4,1024,512]{2,1,0:T(8,128)(2,1)}), bf16[1,1024,512]{2,1,0:T(8,128)(2,1)}) %reduce-scatter.11.cloned.1.call-update) | async-done | bytes 1048592 | tf_op jit(solution)/shard_map/reduce_scatter | solution.py:222
  883.2 2.7 convert_reduce_fusion.1
  885.9 3.1 fusion.41
  889.0 4.2 all-to-all-start.1
  893.3 4.4 fusion.77
  900.1 10.1 all-to-all-done.1
  913.0 41.1 %all-reduce = (f32[512]{0:T(512)}, f32[512]{0:T(512)}, f32[512]{0:T(512)}, f32[512]{0:T(512)}, f32[512]{0:T(512)}, /*index=5*/f32[2048]{0:T(1024)}, f32[512]{0:T(512)}) all-reduce(f32[512]{0:T(512)} %copy-done.32, f32[512]{0:T(512)S(1)} %copy-done.38, f32[512]{0:T(512)S(1)} %copy-done.37, ...), channel_id=1, replica_groups=mesh['dp'=8,'tensor'=4] {'dp','tensor'}, use_global_device_ids=true, to_apply=%region_23.24 | all-reduce | flops 5120 | bytes 40960 | tf_op jit(solution)/shard_map/psum | solution.py:252
  954.1 77.5 %all-reduce.3.cloned.1.call-done = f32[512,512]{1,0:T(8,128)} async-done(((f32[512,512]{1,0:T(8,128)}), f32[512,512]{1,0:T(8,128)}) %all-reduce.3.cloned.1.call-update) | async-done | bytes 1048592 | tf_op jit(solution)/shard_map/psum | solution.py:252
  1031.6 2.3 copy.119
  (238 shorter events, 78.8 us)
Async XLA Ops:
  7.2 1.2 copy-start
  7.2 8.6 copy-start.27
  7.2 8.6 copy-start.21
  7.2 92.1 %all-gather.5.cloned.1.call-start = ((), (), s32[]{:S(2)}) async-start(), calls=%async_computation.6 | async-start | bytes 5242880 | tf_op jit(solution)/shard_map/all_gather | solution.py:152
  8.1 1.0 copy-start.33
  8.1 3.2 copy-start.35
  9.7 290.2 %copy-start.18 = (f32[512]{0:T(512)}, f32[512]{0:T(512)S(1)}, u32[]{:S(2)}) copy-start(f32[512]{0:T(512)S(1)} %add.138) | copy-start | bytes 6148
  11.3 4.6 copy-start.14
  13.0 2.9 copy-start.25
  13.0 2.8 copy-start.22
  15.7 284.2 %reduce-scatter.5.cloned.1.call-start = ((), (), s32[]{:S(2)}) async-start(), calls=%async_computation.7 | async-start | bytes 10485760 | tf_op jit(solution)/shard_map/reduce_scatter | solution.py:160
  36.3 67.6 %copy-start.12 = (bf16[3,512,128]{2,1,0:T(8,128)(2,1)}, bf16[3,512,128]{2,1,0:T(8,128)(2,1)S(1)}, u32[]{:S(2)}) copy-start(bf16[3,512,128]{2,1,0:T(8,128)(2,1)S(1)} %all_gather.25) | copy-start | bytes 1179652
  105.4 4.3 copy-start.20
  105.4 4.3 copy-start.46
  152.2 4.6 copy-start.6
  152.2 4.5 copy-start.7
  152.2 4.5 copy-start.10
  156.8 143.2 %copy-start.2 = (bf16[1,1024,512]{2,1,0:T(8,128)(2,1)S(1)}, bf16[1,1024,512]{2,1,0:T(8,128)(2,1)}, u32[]{:S(2)}) copy-start(bf16[1,1024,512]{2,1,0:T(8,128)(2,1)} %param.21) | copy-start | bytes 3145732
  156.8 145.5 %copy-start.31 = (f32[512]{0:T(512)S(1)}, f32[512]{0:T(512)}, u32[]{:S(2)}) copy-start(f32[512]{0:T(512)} %param.33) | copy-start | bytes 6148
  156.8 145.5 %copy-start.43 = (f32[512]{0:T(512)S(1)}, f32[512]{0:T(512)}, u32[]{:S(2)}) copy-start(f32[512]{0:T(512)} %param.34) | copy-start | bytes 6148
  156.8 228.6 %all-gather.7.cloned.1.call-start = ((), (), s32[]{:S(2)}) async-start(), calls=%async_computation.8 | async-start | bytes 5242880 | tf_op jit(solution)/shard_map/all_gather | solution.py:168
  301.9 2.5 copy-start.16
  301.9 2.5 copy-start.17
  303.7 162.5 %all-gather.9.cloned.1.call-start = ((), (), s32[]{:S(2)}) async-start(), calls=%async_computation.10 | async-start | bytes 5242880 | tf_op jit(solution)/shard_map/all_gather | solution.py:185
  304.3 254.1 %reduce-scatter.9.cloned.1.call-start = ((), (), s32[]{:S(2)}) async-start(), calls=%async_computation.11 | async-start | bytes 5242880 | tf_op jit(solution)/shard_map/reduce_scatter | solution.py:197
  476.5 2.0 copy-start.47
  483.0 155.0 %reduce-scatter.7.cloned.1.call-start = ((), (), s32[]{:S(2)}) async-start(), calls=%async_computation.9 | async-start | bytes 5242880 | tf_op jit(solution)/shard_map/reduce_scatter | solution.py:175
  491.8 146.2 %copy-start.44 = (f32[512]{0:T(512)S(1)}, f32[512]{0:T(512)}, u32[]{:S(2)}) copy-start(f32[512]{0:T(512)} %param.36) | copy-start | bytes 6148
  491.9 233.5 %all-gather.11.cloned.1.call-start = ((), (), s32[]{:S(2)}) async-start(), calls=%async_computation.12 | async-start | bytes 5242880 | tf_op jit(solution)/shard_map/all_gather | solution.py:209
  561.2 81.3 %copy-start.8 = (bf16[1,1024,512]{2,1,0:T(8,128)(2,1)S(1)}, bf16[1,1024,512]{2,1,0:T(8,128)(2,1)}, u32[]{:S(2)}) copy-start(bf16[1,1024,512]{2,1,0:T(8,128)(2,1)} %param.37) | copy-start | bytes 3145732
  641.2 1.3 copy-start.5
  641.2 87.6 %copy-start.24 = (f32[1024]{0:T(1024)}, f32[1024]{0:T(1024)S(1)}, u32[]{:S(2)}) copy-start(f32[1024]{0:T(1024)S(1)} %negate_multiply_fusion.1) | copy-start | bytes 12292
  643.9 239.2 %reduce-scatter.11.cloned.1.call-start = ((), (), s32[]{:S(2)}) async-start(), calls=%async_computation.13 | async-start | bytes 5242880 | tf_op jit(solution)/shard_map/reduce_scatter | solution.py:222
  728.8 72.6 %copy-start.13 = (bf16[3,512,128]{2,1,0:T(8,128)(2,1)S(1)}, bf16[3,512,128]{2,1,0:T(8,128)(2,1)}, u32[]{:S(2)}) copy-start(bf16[3,512,128]{2,1,0:T(8,128)(2,1)} %copy-done.12) | copy-start | bytes 1179652
  801.4 6.3 copy-start.34
  801.4 6.3 copy-start.36
  808.7 0.6 copy-start.28
  809.3 6.5 copy-start.45
  815.8 7.2 copy-start.4
  815.8 7.2 copy-start.11
  825.3 57.9 %copy-start.3 = (bf16[1,1024,512]{2,1,0:T(8,128)(2,1)S(1)}, bf16[1,1024,512]{2,1,0:T(8,128)(2,1)}, u32[]{:S(2)}) copy-start(bf16[1,1024,512]{2,1,0:T(8,128)(2,1)} %param.21) | copy-start | bytes 3145732
  825.3 57.9 %copy-start.15 = (f32[1024]{0:T(1024)S(1)}, f32[1024]{0:T(1024)}, u32[]{:S(2)}) copy-start(f32[1024]{0:T(1024)} %copy-done.14) | copy-start | bytes 12292
  825.3 57.9 %copy-start.19 = (f32[512]{0:T(512)S(1)}, f32[512]{0:T(512)}, u32[]{:S(2)}) copy-start(f32[512]{0:T(512)} %copy-done.18) | copy-start | bytes 6148
  825.3 57.9 %copy-start.30 = (f32[512]{0:T(512)S(1)}, f32[512]{0:T(512)}, u32[]{:S(2)}) copy-start(f32[512]{0:T(512)} %param.31) | copy-start | bytes 6148
  830.4 55.4 %copy-start.26 = (f32[1024]{0:T(1024)S(1)}, f32[1024]{0:T(1024)}, u32[]{:S(2)}) copy-start(f32[1024]{0:T(1024)} %copy-done.25) | copy-start | bytes 12292
  830.4 55.4 %copy-start.23 = (f32[1024]{0:T(1024)S(1)}, f32[1024]{0:T(1024)}, u32[]{:S(2)}) copy-start(f32[1024]{0:T(1024)} %copy-done.22) | copy-start | bytes 12292
  830.7 62.7 %copy-start.9 = (bf16[1,1024,512]{2,1,0:T(8,128)(2,1)S(1)}, bf16[1,1024,512]{2,1,0:T(8,128)(2,1)}, u32[]{:S(2)}) copy-start(bf16[1,1024,512]{2,1,0:T(8,128)(2,1)} %param.37) | copy-start | bytes 3145732
  831.4 57.5 %all-to-all-start = ((bf16[8,3,64,128]{3,2,1,0:T(8,128)(2,1)}), bf16[8,3,64,128]{3,2,1,0:T(8,128)(2,1)S(1)}, u32[]{:S(2)}, u32[]{:S(2)}) async-start(bf16[8,3,64,128]{3,2,1,0:T(8,128)(2,1)} %copy.79), calls=%async_computation.4 | async-start | bytes 786432 | tf_op jit(solution)/shard_map/all_to_all | solution.py:21
  889.0 21.2 %all-to-all-start.1 = ((bf16[8,64,1152]{2,1,0:T(8,128)(2,1)}), bf16[8,64,1152]{2,1,0:T(8,128)(2,1)}, u32[]{:S(2)}, u32[]{:S(2)}) async-start(bf16[8,64,1152]{2,1,0:T(8,128)(2,1)} %bitcast.206), calls=%async_computation.5 | async-start | bytes 2359296 | tf_op jit(solution)/shard_map/all_to_all | solution.py:21
  893.2 138.4 %all-reduce.3.cloned.1.call-start = ((), (), s32[]{:S(2)}) async-start(), calls=%async_computation.14 | async-start | bytes 2097152 | tf_op jit(solution)/shard_map/psum | solution.py:252
  893.3 5.0 copy-start.39
  893.3 140.6 %copy-start.1 = (f32[512,512]{1,0:T(8,128)S(1)}, f32[512,512]{1,0:T(8,128)}, u32[]{:S(2)}) copy-start(f32[512,512]{1,0:T(8,128)} %param.29) | copy-start | bytes 3145732
  897.7 0.6 copy-start.32
  897.7 15.3 %copy-start.29 = (f32[2048]{0:T(1024)S(1)}, f32[2048]{0:T(1024)}, u32[]{:S(2)}) copy-start(f32[2048]{0:T(1024)} %copy-done.28) | copy-start | bytes 24580
  897.7 15.3 %copy-start.37 = (f32[512]{0:T(512)S(1)}, f32[512]{0:T(512)}, u32[]{:S(2)}) copy-start(f32[512]{0:T(512)} %get-tuple-element.163) | copy-start | bytes 6148
  897.7 15.3 %copy-start.38 = (f32[512]{0:T(512)S(1)}, f32[512]{0:T(512)}, u32[]{:S(2)}) copy-start(f32[512]{0:T(512)} %get-tuple-element.160) | copy-start | bytes 6148
  897.7 15.3 %copy-start.40 = (f32[512]{0:T(512)S(1)}, f32[512]{0:T(512)}, u32[]{:S(2)}) copy-start(f32[512]{0:T(512)} %get-tuple-element.158) | copy-start | bytes 6148
  897.7 15.3 %copy-start.41 = (f32[512]{0:T(512)S(1)}, f32[512]{0:T(512)}, u32[]{:S(2)}) copy-start(f32[512]{0:T(512)} %get-tuple-element.162) | copy-start | bytes 6148
  897.7 15.3 %copy-start.42 = (f32[512]{0:T(512)S(1)}, f32[512]{0:T(512)}, u32[]{:S(2)}) copy-start(f32[512]{0:T(512)} %get-tuple-element.224) | copy-start | bytes 6148
Sparse Core Ops, SparseCore 0:
  15.9 83.4 all-gather.4
  156.9 142.9 reduce-scatter.4
  303.9 81.5 all-gather.6
  386.9 79.2 all-gather.8
  483.1 75.2 reduce-scatter.8
  560.7 77.2 reduce-scatter.6
  644.0 81.2 all-gather.10
  807.8 75.2 reduce-scatter.10
  900.7 130.9 all-reduce.2
where the time goes:
time: 1040 us
  waiting for transfers between devices  700 us (67%)
  matrix products  127 us (12%)
  blocking collectives  81.5 us (8%)
  other arithmetic  71.6 us (7%)
  local copies, waits for them, and re-layouts  35.8 us (3%)
  between operations  15.5 us (1%)
    reduce_scatter x1, waiting for transfers between devices, shards(): lax.psum_scatter(jnp.einsum('nse,de->nsd', part_rows, out_copy, preferred...  143 us
    all_gather x1, waiting for transfers between devices, shards(): grad_attn_all = lax.all_gather(grad_attn, 'tensor', axis=0, tiled=True)  81.2 us
    psum x1, waiting for transfers between devices, shards(): lax.psum((grad_time_w, grad_time_bias, grad_gain_one, grad_bias_one, grad...  77.5 us
    reduce_scatter x1, waiting for transfers between devices, shards(): lax.psum_scatter(jnp.einsum('nsf,df->nsd', part_rows, down_copy, preferre...  76.8 us
    all_gather x1, waiting for transfers between devices, shards(): grad_out_all = lax.all_gather(cotangent, 'tensor', axis=0, tiled=True)  72.8 us
    reduce_scatter x1, waiting for transfers between devices, shards(): lax.psum_scatter(jnp.einsum('nsf,df->nsd', part_rows, up_copy, preferred_...  66.5 us
    all_gather x1, waiting for transfers between devices, shards(): normed_all = lax.all_gather(normed_one, 'tensor', axis=0, tiled=True)  63.1 us
    all_gather x1, waiting for transfers between devices, shards(): second_all = lax.all_gather(normed_two, 'tensor', axis=0, tiled=True)  60.2 us
  transfers between devices with their start and end apart: 11, of which 10 were waited for; matrix products, arithmetic and copies ran while one was open for 6% of the time, Pallas kernels for 0%

commit v1 on v0

--- a/solution.py
+++ b/solution.py
@@ -182,7 +182,14 @@
     ).astype(jnp.float32)
     layer_out = (middle + ffn_out + b_down).astype(jnp.bfloat16)
     grad_b_down = jnp.sum(cotangent.astype(jnp.float32), axis=(0, 1))
-    grad_out_all = lax.all_gather(cotangent, "tensor", axis=0, tiled=True)
+    array = cotangent
+    ways, here, lap = (lax.axis_size("tensor"), lax.axis_index("tensor"), array.shape[0])
+    shape = [n * ways if d == 0 else n for d, n in enumerate(array.shape)]
+    full = lax.dynamic_update_slice_in_dim(jnp.zeros(shape, array.dtype), array, here * lap, axis=0)
+    for far in range(1, ways):
+        array = lax.ppermute(array, "tensor", [(d, (d + 1) % ways) for d in range(ways)])
+        full = lax.dynamic_update_slice_in_dim(full, array, (here - far) % ways * lap, axis=0)
+    grad_out_all = full
     grad_down = jnp.einsum(
         "nsd,nsf->df", grad_out_all, activated, preferred_element_type=jnp.float32
     )

time: 1040 us -> 1040 us (level)
  waiting for transfers between devices: 700 us -> 650 us
  starting transfers between devices: 8.57 us -> 40.4 us
    ppermute x0 -> x3, waiting for transfers between devices: none -> 83 us  [shards(): lax.ppermute(array, 'tensor', [(d, (d + 1) % ways) for d in range(ways)])]
    all_gather x1 -> x0, waiting for transfers between devices: 72.8 us -> none  [shards(): grad_out_all = lax.all_gather(cotangent, 'tensor', axis=0, tiled=True)]
    all_gather x1, waiting for transfers between devices: 60.2 us -> 0.01 us  [shards(): second_all = lax.all_gather(normed_two, 'tensor', axis=0, tiled=True)]
    ppermute x0 -> x3, starting transfers between devices: none -> 32.1 us  [shards(): lax.ppermute(array, 'tensor', [(d, (d + 1) % ways) for d in range(ways)])]
  transfers between devices with their start and end apart: 11 -> 13, of which waited for: 10 -> 10; matrix products, arithmetic and copies ran while one was open for 6% -> 6% of each run, Pallas kernels for 0% -> 0%
where the time goes in v1:
time: 1040 us; the launch traced here: 1030 us
  waiting for transfers between devices  650 us (62%)
  matrix products  126 us (12%)
  blocking collectives  83.5 us (8%)
  other arithmetic  72.5 us (7%)
  local copies, waits for them, and re-layouts  45.8 us (4%)
  starting transfers between devices  40.4 us (4%)
  between operations  15.8 us (2%)
    reduce_scatter x1, waiting for transfers between devices, shards(): lax.psum_scatter(jnp.einsum('nse,de->nsd', part_rows, out_copy, preferred...  143 us
    ppermute x3, waiting for transfers between devices, shards(): lax.ppermute(array, 'tensor', [(d, (d + 1) % ways) for d in range(ways)])  83 us
    all_gather x1, waiting for transfers between devices, shards(): grad_attn_all = lax.all_gather(grad_attn, 'tensor', axis=0, tiled=True)  81.2 us
    psum x1, waiting for transfers between devices, shards(): lax.psum((grad_time_w, grad_time_bias, grad_gain_one, grad_bias_one, grad...  77.5 us
    reduce_scatter x1, waiting for transfers between devices, shards(): lax.psum_scatter(jnp.einsum('nsf,df->nsd', part_rows, down_copy, preferre...  76.8 us
    reduce_scatter x1, waiting for transfers between devices, shards(): lax.psum_scatter(jnp.einsum('nsf,df->nsd', part_rows, up_copy, preferred_...  67.2 us
    all_gather x1, waiting for transfers between devices, shards(): normed_all = lax.all_gather(normed_one, 'tensor', axis=0, tiled=True)  63.1 us
    reduce_scatter x1, waiting for transfers between devices, shards(): lax.psum_scatter(jnp.einsum('ncse,cde->nsd', part_rows, qkv_copy, preferr...  47.6 us
  transfers between devices with their start and end apart: 13, of which 10 were waited for; matrix products, arithmetic and copies ran while one was open for 6% of the time, Pallas kernels for 0%

profile of v1, /device:TPU:0, one launch (start us, length us, event | category | flops | bytes accessed | tf_op | source)
XLA Modules:
  0.0 1033.9 jit_solution(12299230444967236747)
XLA Ops:
  13.0 2.7 add_convert_fusion.2
  15.9 10.7 %all_gather.23 = bf16[512,128]{1,0:T(8,128)(2,1)S(1)} all-gather(bf16[64,128]{1,0:T(8,128)(2,1)S(1)} %convert_element_type.130), channel_id=1, replica_groups=mesh['dp'=8,'tensor'=4] {'dp'}, dimensions={0}, use_global_device_ids=true | all-gather | bytes 147456 | tf_op jit(solution)/shard_map/all_gather | solution.py:140
  26.6 9.7 all_gather.22
  36.3 63.1 %all-gather.4.cloned.1.call-done = bf16[4,1024,512]{2,1,0:T(8,128)(2,1)} async-done(((bf16[1,1024,512]{2,1,0:T(8,128)(2,1)}), bf16[4,1024,512]{2,1,0:T(8,128)(2,1)}) %all-gather.4.cloned.1.call-update) | async-done | bytes 4194320 | tf_op jit(solution)/shard_map/all_gather | solution.py:152
  99.4 4.5 convert_bitcast_fusion
  109.8 42.4 %while.22 = (s32[]{:T(128)}, bf16[4,1024,128]{1,2,0:T(8,128)(2,1)S(1)}, f32[4,2,1024,1]{2,1,3,0:T(2,128)S(1)}, bf16[4,1024,128]{1,2,0:T(8,128)(2,1)S(1)}, s32[4,...) while((s32[]{:T(128)}, ...), condition=%wide.region_5.6_spmd, body=%wide.region_2.5_spmd.sunk | while | flops 566361088 | bytes 32585864 | solution.py:156
  115.5 2.0 fusion.134
  117.5 2.8 fusion.135
  126.1 2.0 fusion.134
  128.1 2.8 fusion.135
  136.7 2.0 fusion.134
  138.7 2.8 fusion.135
  147.3 2.0 fusion.134
  149.3 2.8 fusion.135
  152.2 4.5 fusion.68
  156.9 143.1 %reduce-scatter.5.cloned.1.call-done = f32[1,1024,512]{2,1,0:T(8,128)} async-done(((f32[4,1024,512]{2,1,0:T(8,128)}), f32[1,1024,512]{2,1,0:T(8,128)}) %reduce-scatter.5.cloned.1.call-update) | async-done | bytes 2097168 | tf_op jit(solution)/shard_map/reduce_scatter | solution.py:160
  300.0 1.9 fusion.78
  305.1 39.6 %collective-permute-done = bf16[1,1024,512]{2,1,0:T(8,128)(2,1)S(1)} collective-permute-done((bf16[1,1024,512]{2,1,0:T(8,128)(2,1)S(1)}, bf16[1,1024,512]{2,1,0:T(8,128)(2,1)S(1)}, u32[]{:S(2)}, u32[]{:S(2)}) %collective-permute-start) | collective-permute-done | bytes 1048608 | tf_op jit(solution)/shard_map/ppermute | solution.py:190
  345.6 18.6 %collective-permute-start.1 = (bf16[1,1024,512]{2,1,0:T(8,128)(2,1)S(1)}, bf16[1,1024,512]{2,1,0:T(8,128)(2,1)}, u32[]{:S(2)}, u32[]{:S(2)}) collective-permute-start(bf16[1,1024,512]{2,1,0:T(8,128)(2,1)S(1)} %collective-permute-done), channel_id=1, source_target_pairs={{0,1},{1,2},{2,3},{3,0},{4,5},{5,6},{6,7},{7,4},{8,9},{9,10},{10,1... | collective-permute-start | bytes 3145736 | tf_op jit(solution)/shard_map/ppermute | solution.py:190
  364.2 43.4 %collective-permute-done.1 = bf16[1,1024,512]{2,1,0:T(8,128)(2,1)} collective-permute-done((bf16[1,1024,512]{2,1,0:T(8,128)(2,1)S(1)}, bf16[1,1024,512]{2,1,0:T(8,128)(2,1)}, u32[]{:S(2)}, u32[]{:S(2)}) %collective-permute-start.1) | collective-permute-done | bytes 1048608 | tf_op jit(solution)/shard_map/ppermute | solution.py:190
  407.6 12.3 %collective-permute-start.2 = (bf16[1,1024,512]{2,1,0:T(8,128)(2,1)}, bf16[1,1024,512]{2,1,0:T(8,128)(2,1)}, u32[]{:S(2)}, u32[]{:S(2)}) collective-permute-start(bf16[1,1024,512]{2,1,0:T(8,128)(2,1)} %collective-permute-done.1), channel_id=1, source_target_pairs={{0,1},{1,2},{2,3},{3,0},{4,5},{5,6},{6,7},{7,4},{8,9},{9,10},{10,1... | collective-permute-start | bytes 3145736 | tf_op jit(solution)/shard_map/ppermute | solution.py:190
  421.8 11.2 %all_gather.26 = bf16[512,512]{1,0:T(8,128)(2,1)} all-gather(bf16[64,512]{1,0:T(8,128)(2,1)S(1)} %convert_element_type.134), channel_id=1, replica_groups=mesh['dp'=8,'tensor'=4] {'dp'}, dimensions={0}, use_global_device_ids=true | all-gather | bytes 589824 | tf_op jit(solution)/shard_map/all_gather | solution.py:142
  433.0 10.7 %all_gather.25 = bf16[512,512]{1,0:T(8,128)(2,1)} all-gather(bf16[64,512]{1,0:T(8,128)(2,1)S(1)} %convert_element_type.132), channel_id=1, replica_groups=mesh['dp'=8,'tensor'=4] {'dp'}, dimensions={0}, use_global_device_ids=true | all-gather | bytes 589824 | tf_op jit(solution)/shard_map/all_gather | solution.py:141
  443.7 2.3 broadcast_in_dim.53
  448.1 2.3 constant_dynamic-update-slice_fusion.2
  450.4 2.3 constant_dynamic-update-slice_fusion.1
  452.7 4.8 fusion.63
  457.5 11.0 %convert_reduce_fusion = (f32[512]{0:T(512)S(1)}, bf16[4,1024,512]{2,1,0:T(8,128)(2,1)S(1)}) fusion(f32[4,1024,512]{2,1,0:T(8,128)S(1)} %fusion.63, f32[512]{0:T(512)S(1)} %dynamic_slice.43, bf16[4,1024,512]{2,1,0:T(8,128)(2,1)} %constant_dynamic-update-slice_fusion.1, bf16[512,512]{1,0:T(8,128)(2,1)S(1)} %copy-done.16), kind=kOutput, calls=%fused_computation.53 | convolution fusion | flops 2195717632 | bytes 17305600 | tf_op jit(solution)/shard_map/nsd,df->nsf/dot_general | solution.py:196
  468.6 1.9 copy-done.50
  470.5 4.6 convolution_convert_fusion
  475.2 8.9 convolution_convert_fusion.1
  484.1 67.2 %reduce-scatter.9.cloned.1.call-done = bf16[1,1024,512]{2,1,0:T(8,128)(2,1)} async-done(((bf16[4,1024,512]{2,1,0:T(8,128)(2,1)}), bf16[1,1024,512]{2,1,0:T(8,128)(2,1)}) %reduce-scatter.9.cloned.1.call-update) | async-done | bytes 1048592 | tf_op jit(solution)/shard_map/reduce_scatter | solution.py:204
  551.3 2.7 fusion.40
  554.1 76.8 %reduce-scatter.7.cloned.1.call-done = bf16[1,1024,512]{2,1,0:T(8,128)(2,1)} async-done(((bf16[4,1024,512]{2,1,0:T(8,128)(2,1)}), bf16[1,1024,512]{2,1,0:T(8,128)(2,1)}) %reduce-scatter.7.cloned.1.call-update) | async-done | bytes 1048592 | tf_op jit(solution)/shard_map/reduce_scatter | solution.py:175
  630.9 3.2 fusion.77
  637.0 81.2 %all-gather.8.cloned.1.call-done = bf16[4,1024,512]{2,1,0:T(8,128)(2,1)} async-done(((bf16[1,1024,512]{2,1,0:T(8,128)(2,1)}), bf16[4,1024,512]{2,1,0:T(8,128)(2,1)}) %all-gather.8.cloned.1.call-update) | async-done | bytes 4194320 | tf_op jit(solution)/shard_map/all_gather | solution.py:216
  718.2 3.4 convolution_convert_fusion.2
  721.7 72.6 %while.23 = (s32[]{:T(128)}, bf16[4,3,1024,128]{2,3,1,0:T(8,128)(2,1)}, bf16[4,1024,128]{1,2,0:T(8,128)(2,1)}, s32[4,1024]{1,0:T(4,128)S(1)}, s32[4]{0:T(128)S(1...) while((s32[]{:T(128)}, ...), condition=%wide.region_15.16_spmd, body=%wide.region_13.15_spmd.sunk | while | flops 1380842496 | bytes 73996440 | solution.py:221
  728.0 2.5 fusion.148
  730.5 3.4 multiply_reduce_fusion.4
  734.0 2.7 multiply_convert_fusion.5
  746.2 2.5 fusion.148
  748.7 3.4 multiply_reduce_fusion.4
  752.1 2.7 multiply_convert_fusion.5
  764.3 2.5 fusion.148
  766.8 3.4 multiply_reduce_fusion.4
  770.3 2.7 multiply_convert_fusion.5
  782.5 2.5 fusion.148
  785.0 3.4 multiply_reduce_fusion.4
  788.4 2.7 multiply_convert_fusion.5
  794.3 6.3 bitcast_convert_fusion
  802.2 6.2 fusion.47
  808.5 8.1 fusion.48
  818.9 5.1 fusion.56
  825.0 3.5 all-to-all-start
  828.4 47.6 %reduce-scatter.11.cloned.1.call-done = bf16[1,1024,512]{2,1,0:T(8,128)(2,1)} async-done(((bf16[4,1024,512]{2,1,0:T(8,128)(2,1)}), bf16[1,1024,512]{2,1,0:T(8,128)(2,1)}) %reduce-scatter.11.cloned.1.call-update) | async-done | bytes 1048592 | tf_op jit(solution)/shard_map/reduce_scatter | solution.py:229
  876.1 2.7 convert_reduce_fusion.1
  878.8 3.1 fusion.41
  881.9 4.3 all-to-all-start.1
  886.3 4.4 fusion.76
  893.0 10.1 all-to-all-done.1
  905.9 41.1 %all-reduce = (f32[512]{0:T(512)}, f32[512]{0:T(512)}, f32[512]{0:T(512)}, f32[512]{0:T(512)}, f32[512]{0:T(512)}, /*index=5*/f32[2048]{0:T(1024)}, f32[512]{0:T(512)}) all-reduce(f32[512]{0:T(512)} %copy-done.36, f32[512]{0:T(512)S(1)} %copy-done.42, f32[512]{0:T(512)S(1)} %copy-done.41, ...), channel_id=1, replica_groups=mesh['dp'=8,'tensor'=4] {'dp','tensor'}, use_global_device_ids=true, to_apply=%region_23.24 | all-reduce | flops 5120 | bytes 40960 | tf_op jit(solution)/shard_map/psum | solution.py:259
  947.0 77.5 %all-reduce.3.cloned.1.call-done = f32[512,512]{1,0:T(8,128)} async-done(((f32[512,512]{1,0:T(8,128)}), f32[512,512]{1,0:T(8,128)}) %all-reduce.3.cloned.1.call-update) | async-done | bytes 1048592 | tf_op jit(solution)/shard_map/psum | solution.py:259
  1024.6 2.3 copy.123
  (252 shorter events, 92.9 us)
Async XLA Ops:
  7.2 1.2 copy-start
  7.2 8.6 copy-start.31
  7.2 8.6 copy-start.25
  7.2 92.1 %all-gather.4.cloned.1.call-start = ((), (), s32[]{:S(2)}) async-start(), calls=%async_computation.6 | async-start | bytes 5242880 | tf_op jit(solution)/shard_map/all_gather | solution.py:152
  8.1 1.0 copy-start.37
  8.1 3.2 copy-start.39
  9.7 290.2 %copy-start.22 = (f32[512]{0:T(512)}, f32[512]{0:T(512)S(1)}, u32[]{:S(2)}) copy-start(f32[512]{0:T(512)S(1)} %add.163) | copy-start | bytes 6148
  11.3 4.6 copy-start.19
  13.0 2.9 copy-start.29
  13.0 2.8 copy-start.26
  15.7 284.2 %reduce-scatter.5.cloned.1.call-start = ((), (), s32[]{:S(2)}) async-start(), calls=%async_computation.7 | async-start | bytes 10485760 | tf_op jit(solution)/shard_map/reduce_scatter | solution.py:160
  36.3 67.6 %copy-start.17 = (bf16[3,512,128]{2,1,0:T(8,128)(2,1)}, bf16[3,512,128]{2,1,0:T(8,128)(2,1)S(1)}, u32[]{:S(2)}) copy-start(bf16[3,512,128]{2,1,0:T(8,128)(2,1)S(1)} %all_gather.22) | copy-start | bytes 1179652
  105.4 4.3 copy-start.24
  105.4 4.3 copy-start.49
  152.2 4.6 copy-start.6
  152.2 4.6 copy-start.7
  152.2 4.5 copy-start.11
  156.8 143.2 %copy-start.2 = (bf16[1,1024,512]{2,1,0:T(8,128)(2,1)S(1)}, bf16[1,1024,512]{2,1,0:T(8,128)(2,1)}, u32[]{:S(2)}) copy-start(bf16[1,1024,512]{2,1,0:T(8,128)(2,1)} %param.21) | copy-start | bytes 3145732
  156.8 145.5 %copy-start.35 = (f32[512]{0:T(512)S(1)}, f32[512]{0:T(512)}, u32[]{:S(2)}) copy-start(f32[512]{0:T(512)} %param.33) | copy-start | bytes 6148
  156.8 145.5 %copy-start.47 = (f32[512]{0:T(512)S(1)}, f32[512]{0:T(512)}, u32[]{:S(2)}) copy-start(f32[512]{0:T(512)} %param.34) | copy-start | bytes 6148
  156.8 295.9 %all-gather.6.cloned.1.call-start = ((), (), s32[]{:S(2)}) async-start(), calls=%async_computation.8 | async-start | bytes 5242880 | tf_op jit(solution)/shard_map/all_gather | solution.py:168
  301.9 1.9 copy-start.8
  301.9 118.0 %copy-start.21 = (f32[64,512]{1,0:T(8,128)S(1)}, f32[64,512]{1,0:T(8,128)}, u32[]{:S(2)}) copy-start(f32[64,512]{1,0:T(8,128)} %param.27) | copy-start | bytes 393220
  303.8 247.6 %reduce-scatter.9.cloned.1.call-start = ((), (), s32[]{:S(2)}) async-start(), calls=%async_computation.10 | async-start | bytes 5242880 | tf_op jit(solution)/shard_map/reduce_scatter | solution.py:204
  303.8 40.8 %collective-permute-start = (bf16[1,1024,512]{2,1,0:T(8,128)(2,1)S(1)}, bf16[1,1024,512]{2,1,0:T(8,128)(2,1)S(1)}, u32[]{:S(2)}, u32[]{:S(2)}) collective-permute-start(bf16[1,1024,512]{2,1,0:T(8,128)(2,1)S(1)} %copy-done.8), channel_id=1, source_target_pairs={{0,1},{1,2},{2,3},{3,0},{4,5},{5,6},{6,7},{7,4},{8,9},{9,10},{10,1... | collective-permute-start | bytes 3145736 | tf_op jit(solution)/shard_map/ppermute | solution.py:190
  344.6 1.0 copy-start.14
  345.6 62.0 %collective-permute-start.1 = (bf16[1,1024,512]{2,1,0:T(8,128)(2,1)S(1)}, bf16[1,1024,512]{2,1,0:T(8,128)(2,1)}, u32[]{:S(2)}, u32[]{:S(2)}) collective-permute-start(bf16[1,1024,512]{2,1,0:T(8,128)(2,1)S(1)} %collective-permute-done), channel_id=1, source_target_pairs={{0,1},{1,2},{2,3},{3,0},{4,5},{5,6},{6,7},{7,4},{8,9},{9,10},{10,1... | collective-permute-start | bytes 3145736 | tf_op jit(solution)/shard_map/ppermute | solution.py:190
  407.6 42.8 %collective-permute-start.2 = (bf16[1,1024,512]{2,1,0:T(8,128)(2,1)}, bf16[1,1024,512]{2,1,0:T(8,128)(2,1)}, u32[]{:S(2)}, u32[]{:S(2)}) collective-permute-start(bf16[1,1024,512]{2,1,0:T(8,128)(2,1)} %collective-permute-done.1), channel_id=1, source_target_pairs={{0,1},{1,2},{2,3},{3,0},{4,5},{5,6},{6,7},{7,4},{8,9},{9,10},{10,1... | collective-permute-start | bytes 3145736 | tf_op jit(solution)/shard_map/ppermute | solution.py:190
  420.9 26.2 %copy-start.15 = (bf16[1,1024,512]{2,1,0:T(8,128)(2,1)S(1)}, bf16[1,1024,512]{2,1,0:T(8,128)(2,1)}, u32[]{:S(2)}) copy-start(bf16[1,1024,512]{2,1,0:T(8,128)(2,1)} %copy-done.14) | copy-start | bytes 3145732
  452.7 4.8 copy-start.16
  457.5 11.1 %copy-start.10 = (f32[4,1024,512]{2,1,0:T(8,128)}, f32[4,1024,512]{2,1,0:T(8,128)S(1)}, u32[]{:S(2)}) copy-start(f32[4,1024,512]{2,1,0:T(8,128)S(1)} %fusion.63) | copy-start | bytes 25165828
  457.5 13.0 %copy-start.13 = (bf16[512,512]{1,0:T(8,128)(2,1)S(1)}, bf16[512,512]{1,0:T(8,128)(2,1)}, u32[]{:S(2)}) copy-start(bf16[512,512]{1,0:T(8,128)(2,1)} %all_gather.25) | copy-start | bytes 1572868
  468.6 1.9 copy-start.50
  475.1 155.8 %reduce-scatter.7.cloned.1.call-start = ((), (), s32[]{:S(2)}) async-start(), calls=%async_computation.9 | async-start | bytes 5242880 | tf_op jit(solution)/shard_map/reduce_scatter | solution.py:175
  484.0 146.9 %copy-start.48 = (f32[512]{0:T(512)S(1)}, f32[512]{0:T(512)}, u32[]{:S(2)}) copy-start(f32[512]{0:T(512)} %param.36) | copy-start | bytes 6148
  484.1 234.2 %all-gather.8.cloned.1.call-start = ((), (), s32[]{:S(2)}) async-start(), calls=%async_computation.11 | async-start | bytes 5242880 | tf_op jit(solution)/shard_map/all_gather | solution.py:216
  634.1 1.3 copy-start.5
  634.1 87.6 %copy-start.28 = (f32[1024]{0:T(1024)}, f32[1024]{0:T(1024)S(1)}, u32[]{:S(2)}) copy-start(f32[1024]{0:T(1024)S(1)} %negate_multiply_fusion.1) | copy-start | bytes 12292
  636.8 239.3 %reduce-scatter.11.cloned.1.call-start = ((), (), s32[]{:S(2)}) async-start(), calls=%async_computation.12 | async-start | bytes 5242880 | tf_op jit(solution)/shard_map/reduce_scatter | solution.py:229
  721.7 72.6 %copy-start.18 = (bf16[3,512,128]{2,1,0:T(8,128)(2,1)S(1)}, bf16[3,512,128]{2,1,0:T(8,128)(2,1)}, u32[]{:S(2)}) copy-start(bf16[3,512,128]{2,1,0:T(8,128)(2,1)} %copy-done.17) | copy-start | bytes 1179652
  794.3 6.3 copy-start.38
  794.3 6.3 copy-start.40
  801.6 0.6 copy-start.32
  808.5 8.1 copy-start.4
  808.5 8.1 copy-start.12
  818.8 57.2 %copy-start.3 = (bf16[1,1024,512]{2,1,0:T(8,128)(2,1)S(1)}, bf16[1,1024,512]{2,1,0:T(8,128)(2,1)}, u32[]{:S(2)}) copy-start(bf16[1,1024,512]{2,1,0:T(8,128)(2,1)} %param.21) | copy-start | bytes 3145732
  818.8 57.2 %copy-start.20 = (f32[1024]{0:T(1024)S(1)}, f32[1024]{0:T(1024)}, u32[]{:S(2)}) copy-start(f32[1024]{0:T(1024)} %copy-done.19) | copy-start | bytes 12292
  818.8 57.2 %copy-start.23 = (f32[512]{0:T(512)S(1)}, f32[512]{0:T(512)}, u32[]{:S(2)}) copy-start(f32[512]{0:T(512)} %copy-done.22) | copy-start | bytes 6148
  818.8 57.2 %copy-start.34 = (f32[512]{0:T(512)S(1)}, f32[512]{0:T(512)}, u32[]{:S(2)}) copy-start(f32[512]{0:T(512)} %param.31) | copy-start | bytes 6148
  824.0 54.8 %copy-start.30 = (f32[1024]{0:T(1024)S(1)}, f32[1024]{0:T(1024)}, u32[]{:S(2)}) copy-start(f32[1024]{0:T(1024)} %copy-done.29) | copy-start | bytes 12292
  824.0 54.8 %copy-start.27 = (f32[1024]{0:T(1024)S(1)}, f32[1024]{0:T(1024)}, u32[]{:S(2)}) copy-start(f32[1024]{0:T(1024)} %copy-done.26) | copy-start | bytes 12292
  824.2 62.0 %copy-start.9 = (bf16[1,1024,512]{2,1,0:T(8,128)(2,1)S(1)}, bf16[1,1024,512]{2,1,0:T(8,128)(2,1)}, u32[]{:S(2)}) copy-start(bf16[1,1024,512]{2,1,0:T(8,128)(2,1)} %param.37) | copy-start | bytes 3145732
  825.0 56.9 %all-to-all-start = ((bf16[8,3,64,128]{3,2,1,0:T(8,128)(2,1)}), bf16[8,3,64,128]{3,2,1,0:T(8,128)(2,1)S(1)}, u32[]{:S(2)}, u32[]{:S(2)}) async-start(bf16[8,3,64,128]{3,2,1,0:T(8,128)(2,1)} %copy.79), calls=%async_computation.4 | async-start | bytes 786432 | tf_op jit(solution)/shard_map/all_to_all | solution.py:21
  881.9 21.2 %all-to-all-start.1 = ((bf16[8,64,1152]{2,1,0:T(8,128)(2,1)}), bf16[8,64,1152]{2,1,0:T(8,128)(2,1)}, u32[]{:S(2)}, u32[]{:S(2)}) async-start(bf16[8,64,1152]{2,1,0:T(8,128)(2,1)} %bitcast.202), calls=%async_computation.5 | async-start | bytes 2359296 | tf_op jit(solution)/shard_map/all_to_all | solution.py:21
  886.2 138.4 %all-reduce.3.cloned.1.call-start = ((), (), s32[]{:S(2)}) async-start(), calls=%async_computation.13 | async-start | bytes 2097152 | tf_op jit(solution)/shard_map/psum | solution.py:259
  886.2 5.0 copy-start.43
  886.3 140.6 %copy-start.1 = (f32[512,512]{1,0:T(8,128)S(1)}, f32[512,512]{1,0:T(8,128)}, u32[]{:S(2)}) copy-start(f32[512,512]{1,0:T(8,128)} %param.29) | copy-start | bytes 3145732
  890.6 0.6 copy-start.36
  890.6 15.3 %copy-start.33 = (f32[2048]{0:T(1024)S(1)}, f32[2048]{0:T(1024)}, u32[]{:S(2)}) copy-start(f32[2048]{0:T(1024)} %copy-done.32) | copy-start | bytes 24580
  890.6 15.3 %copy-start.41 = (f32[512]{0:T(512)S(1)}, f32[512]{0:T(512)}, u32[]{:S(2)}) copy-start(f32[512]{0:T(512)} %get-tuple-element.163) | copy-start | bytes 6148
  890.6 15.3 %copy-start.42 = (f32[512]{0:T(512)S(1)}, f32[512]{0:T(512)}, u32[]{:S(2)}) copy-start(f32[512]{0:T(512)} %get-tuple-element.160) | copy-start | bytes 6148
  890.6 15.3 %copy-start.44 = (f32[512]{0:T(512)S(1)}, f32[512]{0:T(512)}, u32[]{:S(2)}) copy-start(f32[512]{0:T(512)} %get-tuple-element.158) | copy-start | bytes 6148
  890.6 15.3 %copy-start.45 = (f32[512]{0:T(512)S(1)}, f32[512]{0:T(512)}, u32[]{:S(2)}) copy-start(f32[512]{0:T(512)} %get-tuple-element.162) | copy-start | bytes 6148
  890.7 15.3 %copy-start.46 = (f32[512]{0:T(512)S(1)}, f32[512]{0:T(512)}, u32[]{:S(2)}) copy-start(f32[512]{0:T(512)} %get-tuple-element.224) | copy-start | bytes 6148
Sparse Core Ops, SparseCore 0:
  15.9 83.4 all-gather.3
  156.9 142.9 reduce-scatter.4
  303.9 116.8 all-gather.5
  475.2 76.0 reduce-scatter.8
  553.6 77.2 reduce-scatter.6
  636.9 81.2 all-gather.7
  800.8 75.2 reduce-scatter.10
  893.6 130.9 all-reduce.2
